TPU v7x, 256 devices: a whole 4x4x8 slice. The times are simulated.
256 devices in a mesh: lat: 4 (over y_hi, core), lon: 64 (over y_lo, z, x).
Axes of the slice: x: 4, y: 4 (y_hi: 2, y_lo: 2; y = y_hi * 2 + y_lo), z: 8, core: 2. Of those that a mesh axis runs over, the one named last changes fastest.
Arguments:
- inputs: bfloat16 [8, 24, 768, 192], P(None, 'lat', 'lon'), may hold values from -6 to 6
- cotangent: bfloat16 [8, 24, 768, 192], P(None, 'lat', 'lon'), may hold values from -6 to 6
- qkv_weight: bfloat16 [192, 576], P(None, 'lon'), may hold values from -0.4375 to 0.4375
- proj_weight: bfloat16 [192, 192], P(None, 'lon'), may hold values from -0.4375 to 0.4375
- up_weight: bfloat16 [192, 768], P(None, 'lon'), may hold values from -0.4375 to 0.4375
- down_weight: bfloat16 [768, 192], P(None, 'lon'), may hold values from -0.21875 to 0.21875
- norm_gains: bfloat16 [2, 192], P(None, 'lon'), may hold values from 0.099609375 to 1.8984375
- bias_table: bfloat16 [16, 6, 20736], P(None, None, 'lon'), may hold values from -4 to 304
- type_of: int32 [4, 4], replicated, may hold values from 0 to 15
- region: int32 [8, 24], P(None, 'lat'), may hold values from 0 to 2
Outputs:
- grad_input: bfloat16 [8, 24, 768, 192], P(None, 'lat', 'lon')
- grad_qkv: float32 [192, 576], P(None, 'lon')
- grad_proj: float32 [192, 192], P(None, 'lon')
- grad_up: float32 [192, 768], P(None, 'lon')
- grad_down: float32 [768, 192], P(None, 'lon')
- grad_gains: float32 [2, 192], P(None, 'lon')
- grad_table: float32 [16, 6, 20736], P(None, None, 'lon')
Inputs may be any that keep to these rules, and one draw needn't show every extreme that they name: `type_of`: types may repeat and some may be absent. Attention joins only tokens of a window with equal region ids.
All inputs are finite; a program needn't handle non-finite values.
Results may differ from a plain program's by a relative error of at most 0.015.
Values may be sent and summed in bfloat16 or wider, within the bound.
No kernel may reach another device: no remote copies, remote signals or barrier semaphores. Data moves between devices by JAX's collectives and lax.ppermute only.
A program may use at most 64 MiB of HBM per device.

v0:
```python
import math
import jax
import jax.numpy as jnp
from jax import lax
from jax.sharding import PartitionSpec as P

WPL = 2
WLAT = 6
WLON = 12
WIN = 144


def passed_along(block, axis, distance):
    devices = range(lax.axis_size(axis))
    route = [((i - distance) % len(devices), i) for i in devices]
    return lax.ppermute(block, axis, route)


def layer_norm(values):
    row_mean = jnp.mean(values, axis=-1, keepdims=True)
    centred = values - row_mean
    variance = jnp.mean(centred * centred, axis=-1, keepdims=True)
    inv_std = lax.rsqrt(variance + 1e-05)
    return (centred * inv_std, inv_std)


def norm_back(d_normed, normed, inv_std):
    return inv_std * (
        d_normed
        - jnp.mean(d_normed, axis=-1, keepdims=True)
        - normed * jnp.mean(d_normed * normed, axis=-1, keepdims=True)
    )


def gelu_pair(pre_act):
    cumul = 0.5 * (1.0 + lax.erf(pre_act * 0.7071067811865476))
    density = jnp.exp(-0.5 * pre_act * pre_act) * 0.3989422804014327
    return (pre_act * cumul, cumul + pre_act * density)


def to_windows(column, level_windows, row_windows):
    features = column.shape[-1]
    shaped = column.reshape(level_windows, WPL, row_windows, WLAT, WLON, features)
    return shaped.transpose(0, 2, 1, 3, 4, 5).reshape(level_windows * row_windows * WIN, features)


def from_windows(flat, level_windows, row_windows):
    features = flat.shape[-1]
    shaped = flat.reshape(level_windows, row_windows, WPL, WLAT, WLON, features)
    return shaped.transpose(0, 2, 1, 3, 4, 5).reshape(
        level_windows * WPL, row_windows * WLAT, WLON, features
    )


def region_mask(region_rows, level_windows, row_windows):
    labels = region_rows.reshape(level_windows, WPL, row_windows, WLAT).transpose(0, 2, 1, 3)
    labels = jnp.broadcast_to(labels[..., None], (level_windows, row_windows, WPL, WLAT, WLON))
    labels = labels.reshape(level_windows, row_windows, WIN)
    return labels[..., :, None] == labels[..., None, :]


def roll_block(stacked, forward):
    level_shift = WPL // 2
    stacked = jnp.roll(stacked, -level_shift if forward else level_shift, axis=1)
    row_half = WLAT // 2
    rim_rows = stacked[:, :, :row_half] if forward else stacked[:, :, -row_half:]
    arrived = passed_along(rim_rows, "lat", -1 if forward else 1)
    if forward:
        stacked = jnp.concatenate([stacked[:, :, row_half:], arrived], axis=2)
    else:
        stacked = jnp.concatenate([arrived, stacked[:, :, :-row_half]], axis=2)
    col_half = WLON // 2
    rim_cols = stacked[:, :, :, :col_half] if forward else stacked[:, :, :, -col_half:]
    landed = passed_along(rim_cols, "lon", -1 if forward else 1)
    if forward:
        stacked = jnp.concatenate([stacked[:, :, :, col_half:], landed], axis=3)
    else:
        stacked = jnp.concatenate([landed, stacked[:, :, :, :-col_half]], axis=3)
    return stacked


def column_grads(column, cot_column, weights, bias_pos, same_region):
    qkv_full, proj_full, up_full, down_full, gains_full = weights
    f32 = jnp.float32
    bf16 = jnp.bfloat16
    level_windows = column.shape[0] // WPL
    row_windows = column.shape[1] // WLAT
    features = column.shape[-1]
    head_count = bias_pos.shape[2]
    head_size = features // head_count
    factor = 1.0 / math.sqrt(head_size)
    gain_one = gains_full[0].astype(f32)
    gain_two = gains_full[1].astype(f32)
    window_cells = to_windows(column, level_windows, row_windows).astype(f32)
    normed_one, inv_one = layer_norm(window_cells)
    scaled_one = (normed_one * gain_one).astype(bf16)
    packed = jnp.dot(scaled_one, qkv_full, preferred_element_type=f32).astype(bf16)
    packed = packed.reshape(level_windows, row_windows, WIN, 3, head_count, head_size)
    queries = packed[:, :, :, 0]
    key_rows = packed[:, :, :, 1]
    value_rows = packed[:, :, :, 2]
    scores = (
        jnp.einsum("abthd,abshd->abhts", queries, key_rows, preferred_element_type=f32) * factor
    )
    scores = scores + bias_pos.astype(f32)
    scores = jnp.where(same_region[:, :, None], scores, -jnp.inf)
    peak_score = jnp.max(scores, axis=-1, keepdims=True)
    raised = jnp.exp(scores - peak_score)
    attn_probs = raised / jnp.sum(raised, axis=-1, keepdims=True)
    probs_b = attn_probs.astype(bf16)
    attended = jnp.einsum("abhts,abshd->abthd", probs_b, value_rows, preferred_element_type=f32)
    attended = attended.astype(bf16).reshape(-1, features)
    middle = window_cells + jnp.dot(attended, proj_full, preferred_element_type=f32)
    normed_two, inv_two = layer_norm(middle)
    scaled_two = (normed_two * gain_two).astype(bf16)
    pre_act = jnp.dot(scaled_two, up_full, preferred_element_type=f32)
    activated, gelu_slope = gelu_pair(pre_act)
    hidden_b = activated.astype(bf16)
    cot_rows = to_windows(cot_column, level_windows, row_windows)
    grad_down = jnp.dot(hidden_b.T, cot_rows, preferred_element_type=f32)
    d_hidden = (jnp.dot(cot_rows, down_full.T, preferred_element_type=f32) * gelu_slope).astype(
        bf16
    )
    grad_up = jnp.dot(scaled_two.T, d_hidden, preferred_element_type=f32)
    d_htwo = jnp.dot(d_hidden, up_full.T, preferred_element_type=f32)
    gain_grad_two = jnp.sum(d_htwo * normed_two, axis=0)
    d_middle = cot_rows.astype(f32) + norm_back(d_htwo * gain_two, normed_two, inv_two)
    d_middle_b = d_middle.astype(bf16)
    grad_proj = jnp.dot(attended.T, d_middle_b, preferred_element_type=f32)
    d_att = jnp.dot(d_middle_b, proj_full.T, preferred_element_type=f32).astype(bf16)
    d_att = d_att.reshape(level_windows, row_windows, WIN, head_count, head_size)
    d_prob = jnp.einsum("abthd,abshd->abhts", d_att, value_rows, preferred_element_type=f32)
    d_values = jnp.einsum("abhts,abthd->abshd", probs_b, d_att, preferred_element_type=f32)
    d_score = attn_probs * (d_prob - jnp.sum(attn_probs * d_prob, axis=-1, keepdims=True))
    d_score_b = d_score.astype(bf16)
    d_queries = (
        jnp.einsum("abhts,abshd->abthd", d_score_b, key_rows, preferred_element_type=f32) * factor
    )
    d_keys = (
        jnp.einsum("abhts,abthd->abshd", d_score_b, queries, preferred_element_type=f32) * factor
    )
    d_packed = (
        jnp.stack([d_queries, d_keys, d_values], axis=3).astype(bf16).reshape(-1, 3 * features)
    )
    grad_qkv = jnp.dot(scaled_one.T, d_packed, preferred_element_type=f32)
    d_hone = jnp.dot(d_packed, qkv_full.T, preferred_element_type=f32)
    gain_grad_one = jnp.sum(d_hone * normed_one, axis=0)
    d_cells = d_middle + norm_back(d_hone * gain_one, normed_one, inv_one)
    d_column = from_windows(d_cells.astype(bf16), level_windows, row_windows)
    param_grads = (
        grad_qkv,
        grad_proj,
        grad_up,
        grad_down,
        jnp.stack([gain_grad_one, gain_grad_two]),
    )
    table_grad = d_score.reshape(level_windows * row_windows, head_count, WIN * WIN)
    return (d_column, param_grads, table_grad)


def shards(
    inputs,
    cotangent,
    qkv_weight,
    proj_weight,
    up_weight,
    down_weight,
    norm_gains,
    bias_table,
    type_of,
    region,
):
    level_windows = inputs.shape[0] // WPL
    row_windows = inputs.shape[1] // WLAT
    lon_windows = inputs.shape[2] // WLON
    features = inputs.shape[3]
    type_count = bias_table.shape[0]
    head_count = bias_table.shape[1]
    positions = level_windows * row_windows
    lat_index = lax.axis_index("lat")
    type_rows = lax.dynamic_slice(
        type_of, (jnp.int32(0), lat_index * row_windows), (level_windows, row_windows)
    ).reshape(-1)
    onehot = type_rows[:, None] == jnp.arange(type_count, dtype=jnp.int32)[None, :]
    select_half = onehot.astype(jnp.bfloat16)
    select_full = onehot.astype(jnp.float32)
    table_part = bias_table.reshape(type_count * head_count, -1)
    qkv_full, proj_full, up_full, down_full, gains_full, table_full = (
        lax.all_gather(qkv_weight, "lon", axis=1, tiled=True),
        lax.all_gather(proj_weight, "lon", axis=1, tiled=True),
        lax.all_gather(up_weight, "lon", axis=1, tiled=True),
        lax.all_gather(down_weight, "lon", axis=1, tiled=True),
        lax.all_gather(norm_gains, "lon", axis=1, tiled=True),
        lax.all_gather(table_part, "lon", axis=1, tiled=True),
    )
    chosen_rows = jnp.dot(
        select_half, table_full.reshape(type_count, -1), preferred_element_type=jnp.float32
    )
    bias_pos = chosen_rows.astype(jnp.bfloat16).reshape(
        level_windows, row_windows, head_count, WIN, WIN
    )
    same_region = region_mask(region, level_windows, row_windows)
    shifted = roll_block(jnp.stack([inputs, cotangent]), True)
    columns = shifted.reshape(2, inputs.shape[0], inputs.shape[1], lon_windows, WLON, features)
    columns = columns.transpose(3, 0, 1, 2, 4, 5)
    weights = (qkv_full, proj_full, up_full, down_full, gains_full)

    def advance(totals, column_pair):
        d_column, param_grads, table_grad = column_grads(
            column_pair[0], column_pair[1], weights, bias_pos, same_region
        )
        return (jax.tree.map(jnp.add, totals, (param_grads, table_grad)), d_column)

    initial = (
        tuple((jnp.zeros(member.shape, jnp.float32) for member in weights)),
        jnp.zeros((positions, head_count, WIN * WIN), jnp.float32),
    )
    totals, d_columns = lax.scan(advance, initial, columns)
    d_shifted = d_columns.transpose(1, 2, 0, 3, 4).reshape(inputs.shape)
    grad_input = roll_block(d_shifted[None], False)[0]
    param_grads, table_sum = totals
    table_member = jnp.dot(
        select_full.T, table_sum.reshape(positions, -1), precision=lax.Precision.HIGHEST
    ).reshape(type_count * head_count, -1)
    summed = (
        lax.psum_scatter(param_grads[0], "lon", scatter_dimension=1, tiled=True),
        lax.psum_scatter(param_grads[1], "lon", scatter_dimension=1, tiled=True),
        lax.psum_scatter(param_grads[2], "lon", scatter_dimension=1, tiled=True),
        lax.psum_scatter(param_grads[3], "lon", scatter_dimension=1, tiled=True),
        lax.psum_scatter(param_grads[4], "lon", scatter_dimension=1, tiled=True),
        lax.psum_scatter(table_member, "lon", scatter_dimension=1, tiled=True),
    )
    table_shard = summed[5]
    lat_sums = (
        lax.psum(summed[0].astype(jnp.bfloat16), "lat").astype(jnp.float32),
        lax.psum(summed[1].astype(jnp.bfloat16), "lat").astype(jnp.float32),
        lax.psum(summed[2].astype(jnp.bfloat16), "lat").astype(jnp.float32),
        lax.psum(summed[3].astype(jnp.bfloat16), "lat").astype(jnp.float32),
        lax.psum(summed[4].astype(jnp.bfloat16), "lat").astype(jnp.float32),
        lax.psum(table_shard.astype(jnp.bfloat16), "lat").astype(jnp.float32),
    )
    token_count = (
        inputs.shape[0]
        * inputs.shape[1]
        * inputs.shape[2]
        * lax.axis_size("lat")
        * lax.axis_size("lon")
    )
    factor = 1.0 / math.sqrt(token_count)
    return (
        grad_input,
        lat_sums[0] * factor,
        lat_sums[1] * factor,
        lat_sums[2] * factor,
        lat_sums[3] * factor,
        lat_sums[4] * factor,
        lat_sums[5].reshape(type_count, head_count, -1),
    )


def solution(mesh):
    return jax.shard_map(
        shards,
        mesh=mesh,
        in_specs=(
            P(None, "lat", "lon", None),
            P(None, "lat", "lon", None),
            P(None, "lon"),
            P(None, "lon"),
            P(None, "lon"),
            P(None, "lon"),
            P(None, "lon"),
            P(None, None, "lon"),
            P(),
            P(None, "lat"),
        ),
        out_specs=(
            P(None, "lat", "lon", None),
            P(None, "lon"),
            P(None, "lon"),
            P(None, "lon"),
            P(None, "lon"),
            P(None, "lon"),
            P(None, None, "lon"),
        ),
        check_vma=False,
    )
```

profile of v0, /device:TPU:1, one launch (start us, length us, event | category | flops | bytes accessed | tf_op | source)
XLA Modules:
  0.0 1554.6 jit_solution(2564097191101022794)
XLA Ops:
  17.5 131.0 %all-gather = bf16[64,3,2]{1,2,0:T(2,128)(2,1)S(1)} all-gather(bf16[1,3,2]{1,2,0:T(2,128)(2,1)S(1)} %bitcast.129), channel_id=1, replica_groups=mesh['lat'=4,'lon'=64] {'lon'}, dimensions={0}, use_global_device_ids=true | all-gather | bytes 780 | tf_op jit(solution)/shard_map/all_gather | solution.py:193
  148.9 127.0 %all-gather.3 = bf16[64,3,192]{2,1,0:T(4,128)(2,1)S(1)} all-gather(bf16[1,3,192]{2,1,0:T(4,128)(2,1)S(1)} %bitcast.127), channel_id=1, replica_groups=mesh['lat'=4,'lon'=64] {'lon'}, dimensions={0}, use_global_device_ids=true | all-gather | bytes 74880 | tf_op jit(solution)/shard_map/all_gather | solution.py:190
  276.6 127.6 %all-gather.4 = bf16[64,3,768]{2,1,0:T(4,128)(2,1)S(1)} all-gather(bf16[1,3,768]{2,1,0:T(4,128)(2,1)S(1)} %bitcast.124), channel_id=1, replica_groups=mesh['lat'=4,'lon'=64] {'lon'}, dimensions={0}, use_global_device_ids=true | all-gather | bytes 299520 | tf_op jit(solution)/shard_map/all_gather | solution.py:192
  405.1 124.9 %all-gather.1 = bf16[64,9,192]{2,1,0:T(8,128)(2,1)S(1)} all-gather(bf16[1,9,192]{2,1,0:T(8,128)(2,1)S(1)} %bitcast.122), channel_id=1, replica_groups=mesh['lat'=4,'lon'=64] {'lon'}, dimensions={0}, use_global_device_ids=true | all-gather | bytes 224640 | tf_op jit(solution)/shard_map/all_gather | solution.py:189
  530.2 126.4 %all-gather.5 = bf16[64,12,192]{2,1,0:T(8,128)(2,1)S(1)} all-gather(bf16[1,12,192]{2,1,0:T(8,128)(2,1)S(1)} %bitcast.123), channel_id=1, replica_groups=mesh['lat'=4,'lon'=64] {'lon'}, dimensions={0}, use_global_device_ids=true | all-gather | bytes 299520 | tf_op jit(solution)/shard_map/all_gather | solution.py:191
  659.7 5.6 collective-permute-done.1
  672.1 6.3 copy.70
  678.4 9.6 reshape.312
  688.0 7.4 reshape.296
  695.5 4.2 fusion.2
  699.6 4.7 reshape.305
  704.4 3.6 copy.71
  724.9 134.0 %fusion = f32[192,16]{0,1:T(8,128)S(1)} fusion(f32[192,768]{0,1:T(8,128)S(1)} %fusion.35), kind=kCustom, calls=%all-reduce-scatter | all-reduce-scatter fusion | flops 196609 | bytes 603136
  870.1 5.0 convolution_bitcast_fusion
  885.9 4.7 reshape.299
  900.0 5.8 fusion.31
  905.9 6.2 reshape.300
  912.1 314.7 %all-reduce.13 = (bf16[96,20736]{1,0:T(8,128)(2,1)}, bf16[192,576]{0,1:T(8,128)(2,1)S(1)}, bf16[192,192]{0,1:T(8,128)(2,1)S(1)}, bf16[768,192]{0,1:T(8,128)(2,1)}, bf16[2,192]{1,0:T(2,128)(2,1)S(1)}) all-reduce(f32[96,20736]{1,0:T(8,128)} %reshape.300, ...), channel_id=7, replica_groups=mesh['lat'=4,'lon'=64] {'lon'}, use_global_device_ids=true, to_apply=%region_23.24.clone | all-reduce | flops 2285952 | bytes 13715712
  1233.8 17.3 %collective-permute-start.12 = (bf16[192,16]{0,1:T(8,128)(2,1)}, bf16[192,16]{0,1:T(8,128)(2,1)S(1)}, u32[]{:S(2)}, u32[]{:S(2)}) collective-permute-start(bf16[192,16]{0,1:T(8,128)(2,1)} %convert.35), channel_id=1, source_target_pairs={{0,9},{1,10},{2,11},{3,12},{4,13},{5,14},{6,15},{7,16},{8,17},{9,1... | collective-permute-start | bytes 18440
  1251.2 6.6 collective-permute-start.13
  1271.9 4.6 concatenate.34
  1277.1 213.3 %collective-permute-start.2 = (bf16[1,8,3,12,192]{4,3,2,1,0:T(8,128)(2,1)S(1)}, bf16[1,8,3,12,192]{4,3,2,1,0:T(8,128)(2,1)S(1)}, u32[]{:S(2)}, u32[]{:S(2)}) collective-permute-start(bf16[1,8,3,12,192]{4,3,2,1,0:T(8,128)(2,1)S(1)} %fusion.27), channel_id=1, source_target_pairs={{192,0},{0,64},{64,128},{128,192},{193,1},{1,65},{65,129},{129,193... | collective-permute-start | bytes 331784 | tf_op jit(solution)/shard_map/ppermute | solution.py:16
  1490.4 39.8 %all-reduce.12.cloned.1.call-done = (bf16[16,6,324]{2,1,0:T(8,128)(2,1)}, bf16[192,9]{0,1:T(8,128)(2,1)}, bf16[192,3]{0,1:T(4,128)(2,1)}, bf16[192,12]{0,1:T(8,1...) async-done(((bf16[16,6,324]{2,1,0:T(8,128)(2,1)}, bf16[192,9]{0,1:T(8,128)(2,1)}, bf16[192,3]{0,1:T(4,128)(2,1)}, bf16[192,12]{0,1:T(8,128)(2,1)}, ...) | async-done | bytes 76060 | tf_op jit(solution)/shard_map/psum | solution.py:240
  1539.6 6.7 collective-permute-done.3
  (217 shorter events, 99.6 us)
Async XLA Ops:
  7.2 651.1 %copy-start = (s32[4,4]{1,0:T(4,128)S(1)}, s32[4,4]{1,0:T(4,128)}, u32[]{:S(2)}) copy-start(s32[4,4]{1,0:T(4,128)} %param.18) | copy-start | bytes 196
  7.2 664.9 %all-gather.8.cloned.1.call-start = ((), (), s32[]{:S(2)}) async-start(), calls=%async_computation | async-start | bytes 4792320 | tf_op jit(solution)/shard_map/all_gather | solution.py:194
  8.9 1521.3 %all-reduce.12.cloned.1.call-start = ((), (), s32[]{:S(2)}) async-start(), calls=%async_computation.1 | async-start | bytes 246784 | tf_op jit(solution)/shard_map/psum | solution.py:240
  9.0 521.3 %copy-start.31 = (bf16[192,12]{0,1:T(8,128)(2,1)S(1)}, bf16[192,12]{0,1:T(8,128)(2,1)}, u32[]{:S(2)}) copy-start(bf16[192,12]{0,1:T(8,128)(2,1)} %param.14) | copy-start | bytes 13828
  11.6 647.7 %collective-permute-start = (bf16[2,8,3,12,192]{4,1,3,2,0:T(8,128)(2,1)S(1)}, bf16[2,8,3,12,192]{4,1,3,2,0:T(8,128)(2,1)S(1)}, u32[]{:S(2)}, u32[]{:S(2)}) collective-permute-start(bf16[2,8,3,12,192]{4,1,3,2,0:T(8,128)(2,1)S(1)} %get-tuple-element.93), channel_id=1, source_target_pairs={{64,0},{128,64},{192,128},{0,192},{65,1},{129,65},{193,129},{1,193... | collective-permute-start | bytes 663560 | tf_op jit(solution)/shard_map/ppermute | solution.py:16
  659.4 5.9 collective-permute-start.1
  860.1 371.1 %collective-permute-start.5 = (bf16[192,16]{0,1:T(8,128)(2,1)}, bf16[192,16]{0,1:T(8,128)(2,1)}, u32[]{:S(2)}, u32[]{:S(2)}) collective-permute-start(bf16[192,16]{0,1:T(8,128)(2,1)} %convert.35), channel_id=1, source_target_pairs={{0,2},{1,3},{2,4},{3,5},{4,6},{5,7},{6,8},{7,9},{8,10},{9,11},{10,... | collective-permute-start | bytes 18440
  862.0 370.5 %collective-permute-start.6 = (bf16[192,16]{0,1:T(8,128)(2,1)}, bf16[192,16]{0,1:T(8,128)(2,1)}, u32[]{:S(2)}, u32[]{:S(2)}) collective-permute-start(bf16[192,16]{0,1:T(8,128)(2,1)} %convert.35), channel_id=1, source_target_pairs={{0,3},{1,4},{2,5},{3,6},{4,7},{5,8},{6,9},{7,10},{8,11},{9,12},{10... | collective-permute-start | bytes 18440
  863.9 370.0 %collective-permute-start.7 = (bf16[192,16]{0,1:T(8,128)(2,1)}, bf16[192,16]{0,1:T(8,128)(2,1)}, u32[]{:S(2)}, u32[]{:S(2)}) collective-permute-start(bf16[192,16]{0,1:T(8,128)(2,1)} %convert.35), channel_id=1, source_target_pairs={{0,4},{1,5},{2,6},{3,7},{4,8},{5,9},{6,10},{7,11},{8,12},{9,13},{1... | collective-permute-start | bytes 18440
  865.7 385.5 %collective-permute-start.8 = (bf16[192,16]{0,1:T(8,128)(2,1)}, bf16[192,16]{0,1:T(8,128)(2,1)}, u32[]{:S(2)}, u32[]{:S(2)}) collective-permute-start(bf16[192,16]{0,1:T(8,128)(2,1)} %convert.35), channel_id=1, source_target_pairs={{0,5},{1,6},{2,7},{3,8},{4,9},{5,10},{6,11},{7,12},{8,13},{9,14},{... | collective-permute-start | bytes 18440
  884.3 344.3 %collective-permute-start.19 = (bf16[192,12]{0,1:T(8,128)(2,1)}, bf16[192,12]{0,1:T(8,128)(2,1)S(1)}, u32[]{:S(2)}, u32[]{:S(2)}) collective-permute-start(bf16[192,12]{0,1:T(8,128)(2,1)} %slice.107), channel_id=1, source_target_pairs={{0,16},{1,17},{2,18},{3,19},{4,20},{5,21},{6,22},{7,23},{8,24},{9,... | collective-permute-start | bytes 13832
  1228.6 29.2 %collective-permute-start.9 = (bf16[192,16]{0,1:T(8,128)(2,1)}, bf16[192,16]{0,1:T(8,128)(2,1)S(1)}, u32[]{:S(2)}, u32[]{:S(2)}) collective-permute-start(bf16[192,16]{0,1:T(8,128)(2,1)} %convert.35), channel_id=1, source_target_pairs={{0,6},{1,7},{2,8},{3,9},{4,10},{5,11},{6,12},{7,13},{8,14},{9,15},... | collective-permute-start | bytes 18440
  1231.2 28.4 %collective-permute-start.10 = (bf16[192,16]{0,1:T(8,128)(2,1)}, bf16[192,16]{0,1:T(8,128)(2,1)S(1)}, u32[]{:S(2)}, u32[]{:S(2)}) collective-permute-start(bf16[192,16]{0,1:T(8,128)(2,1)} %convert.35), channel_id=1, source_target_pairs={{0,7},{1,8},{2,9},{3,10},{4,11},{5,12},{6,13},{7,14},{8,15},{9,16}... | collective-permute-start | bytes 18440
  1232.5 28.4 %collective-permute-start.11 = (bf16[192,16]{0,1:T(8,128)(2,1)}, bf16[192,16]{0,1:T(8,128)(2,1)S(1)}, u32[]{:S(2)}, u32[]{:S(2)}) collective-permute-start(bf16[192,16]{0,1:T(8,128)(2,1)} %convert.35), channel_id=1, source_target_pairs={{0,8},{1,9},{2,10},{3,11},{4,12},{5,13},{6,14},{7,15},{8,16},{9,17... | collective-permute-start | bytes 18440
  1233.8 29.2 %collective-permute-start.12 = (bf16[192,16]{0,1:T(8,128)(2,1)}, bf16[192,16]{0,1:T(8,128)(2,1)S(1)}, u32[]{:S(2)}, u32[]{:S(2)}) collective-permute-start(bf16[192,16]{0,1:T(8,128)(2,1)} %convert.35), channel_id=1, source_target_pairs={{0,9},{1,10},{2,11},{3,12},{4,13},{5,14},{6,15},{7,16},{8,17},{9,1... | collective-permute-start | bytes 18440
  1251.2 13.7 collective-permute-start.13
  1257.8 9.7 collective-permute-start.14
  1259.7 12.1 collective-permute-start.15
  1261.0 10.8 collective-permute-start.16
  1263.0 8.8 collective-permute-start.17
  1265.0 6.9 collective-permute-start.18
  1267.5 4.3 collective-permute-start.4
  1277.1 258.3 %collective-permute-start.2 = (bf16[1,8,3,12,192]{4,3,2,1,0:T(8,128)(2,1)S(1)}, bf16[1,8,3,12,192]{4,3,2,1,0:T(8,128)(2,1)S(1)}, u32[]{:S(2)}, u32[]{:S(2)}) collective-permute-start(bf16[1,8,3,12,192]{4,3,2,1,0:T(8,128)(2,1)S(1)} %fusion.27), channel_id=1, source_target_pairs={{192,0},{0,64},{64,128},{128,192},{193,1},{1,65},{65,129},{129,193... | collective-permute-start | bytes 331784 | tf_op jit(solution)/shard_map/ppermute | solution.py:16
  1535.6 10.7 collective-permute-start.3
  (38 other events, 2545.0 us)
Sparse Core Ops, SparseCore 0:
  9.9 267.2 all-gather.7
  1277.2 253.0 all-reduce.11
where the time goes:
time: 1560 us; the launch traced here: 1550 us
  blocking collectives  1090 us (70%)
  starting transfers between devices  267 us (17%)
  local copies, waits for them, and re-layouts  77.9 us (5%)
  waiting for transfers between devices  52.2 us (3%)
  matrix products  36.5 us (2%)
  between operations  18 us (1%)
  other arithmetic  17.4 us (1%)
    unnamed x2, blocking collectives  449 us
    ppermute x4, starting transfers between devices, passed_along(): return lax.ppermute(block, axis, route)  218 us
    all_gather x1, blocking collectives, shards(): lax.all_gather(norm_gains, 'lon', axis=1, tiled=True)  131 us
    all_gather x1, blocking collectives, shards(): lax.all_gather(down_weight, 'lon', axis=1, tiled=True)  128 us
    all_gather x1, blocking collectives, shards(): lax.all_gather(proj_weight, 'lon', axis=1, tiled=True)  127 us
    all_gather x1, blocking collectives, shards(): lax.all_gather(up_weight, 'lon', axis=1, tiled=True)  126 us
    all_gather x1, blocking collectives, shards(): lax.all_gather(qkv_weight, 'lon', axis=1, tiled=True)  125 us
    unnamed x16, starting transfers between devices  48.6 us
  transfers between devices with their start and end apart: 22, of which 3 were waited for; matrix products, arithmetic and copies ran while one was open for 4% of the time, Pallas kernels for 0%

commit v1 on v0

--- a/solution.py
+++ b/solution.py
@@ -187,7 +187,9 @@
     table_part = bias_table.reshape(type_count * head_count, -1)
     qkv_full, proj_full, up_full, down_full, gains_full, table_full = (
         lax.all_gather(qkv_weight, "lon", axis=1, tiled=True),
-        lax.all_gather(proj_weight, "lon", axis=1, tiled=True),
+        jnp.concatenate(
+            lax.all_to_all(jnp.stack([proj_weight] * lax.axis_size("lon")), "lon", 0, 0), axis=1
+        ),
         lax.all_gather(up_weight, "lon", axis=1, tiled=True),
         lax.all_gather(down_weight, "lon", axis=1, tiled=True),
         lax.all_gather(norm_gains, "lon", axis=1, tiled=True),

time: 1560 us -> 1430 us (0.917)
  blocking collectives: 1090 us -> 959 us
    all_gather x1 -> x0, blocking collectives: 127 us -> none  [shards(): lax.all_gather(proj_weight, 'lon', axis=1, tiled=True)]
    ppermute x4, starting transfers between devices: 218 us -> 189 us  [passed_along(): return lax.ppermute(block, axis, route)]
  transfers between devices with their start and end apart: 22 -> 23, of which waited for: 3 -> 3; matrix products, arithmetic and copies ran while one was open for 4% -> 5% of each run, Pallas kernels for 0% -> 0%
where the time goes in v1:
time: 1430 us; the launch traced here: 1420 us
  blocking collectives  959 us (67%)
  starting transfers between devices  254 us (18%)
  local copies, waits for them, and re-layouts  79.3 us (6%)
  waiting for transfers between devices  50.9 us (4%)
  matrix products  36.6 us (3%)
  between operations  18 us (1%)
  other arithmetic  17.5 us (1%)
    unnamed x2, blocking collectives  448 us
    ppermute x4, starting transfers between devices, passed_along(): return lax.ppermute(block, axis, route)  189 us
    all_gather x1, blocking collectives, shards(): lax.all_gather(norm_gains, 'lon', axis=1, tiled=True)  129 us
    all_gather x1, blocking collectives, shards(): lax.all_gather(down_weight, 'lon', axis=1, tiled=True)  129 us
    all_gather x1, blocking collectives, shards(): lax.all_gather(qkv_weight, 'lon', axis=1, tiled=True)  127 us
    all_gather x1, blocking collectives, shards(): lax.all_gather(up_weight, 'lon', axis=1, tiled=True)  126 us
    unnamed x16, starting transfers between devices  51.2 us
    psum x1, waiting for transfers between devices, shards(): lax.psum(table_shard.astype(jnp.bfloat16), 'lat').astype(jnp.float32)  39.8 us
  transfers between devices with their start and end apart: 23, of which 3 were waited for; matrix products, arithmetic and copies ran while one was open for 5% of the time, Pallas kernels for 0%

profile of v1, /device:TPU:1, one launch (start us, length us, event | category | flops | bytes accessed | tf_op | source)
XLA Modules:
  0.0 1415.6 jit_solution(18100921978384626069)
XLA Ops:
  10.3 13.6 all-to-all-start
  30.2 129.4 %all-gather = bf16[64,3,2]{1,2,0:T(2,128)(2,1)S(1)} all-gather(bf16[1,3,2]{1,2,0:T(2,128)(2,1)S(1)} %bitcast.129), channel_id=1, replica_groups=mesh['lat'=4,'lon'=64] {'lon'}, dimensions={0}, use_global_device_ids=true | all-gather | bytes 780 | tf_op jit(solution)/shard_map/all_gather | solution.py:195
  159.9 129.1 %all-gather.3 = bf16[64,3,768]{2,1,0:T(4,128)(2,1)S(1)} all-gather(bf16[1,3,768]{2,1,0:T(4,128)(2,1)S(1)} %bitcast.125), channel_id=1, replica_groups=mesh['lat'=4,'lon'=64] {'lon'}, dimensions={0}, use_global_device_ids=true | all-gather | bytes 299520 | tf_op jit(solution)/shard_map/all_gather | solution.py:194
  290.0 126.5 %all-gather.1 = bf16[64,9,192]{2,1,0:T(8,128)(2,1)S(1)} all-gather(bf16[1,9,192]{2,1,0:T(8,128)(2,1)S(1)} %bitcast.123), channel_id=1, replica_groups=mesh['lat'=4,'lon'=64] {'lon'}, dimensions={0}, use_global_device_ids=true | all-gather | bytes 224640 | tf_op jit(solution)/shard_map/all_gather | solution.py:189
  416.8 125.8 %all-gather.4 = bf16[64,12,192]{2,1,0:T(8,128)(2,1)S(1)} all-gather(bf16[1,12,192]{2,1,0:T(8,128)(2,1)S(1)} %bitcast.124), channel_id=1, replica_groups=mesh['lat'=4,'lon'=64] {'lon'}, dimensions={0}, use_global_device_ids=true | all-gather | bytes 299520 | tf_op jit(solution)/shard_map/all_gather | solution.py:193
  546.9 4.3 collective-permute-done.1
  558.0 6.3 copy.71
  564.3 9.6 reshape.322
  573.9 7.4 reshape.304
  585.5 4.7 reshape.315
  610.8 133.8 %fusion = f32[192,16]{0,1:T(8,128)S(1)} fusion(f32[192,768]{0,1:T(8,128)S(1)} %fusion.35), kind=kCustom, calls=%all-reduce-scatter | all-reduce-scatter fusion | flops 196609 | bytes 603136
  755.8 5.0 convolution_bitcast_fusion
  770.0 6.1 collective-permute-start.19
  776.0 4.7 reshape.309
  790.2 5.8 fusion.31
  796.0 6.2 reshape.310
  802.2 314.5 %all-reduce.13 = (bf16[96,20736]{1,0:T(8,128)(2,1)}, bf16[192,576]{0,1:T(8,128)(2,1)S(1)}, bf16[192,192]{0,1:T(8,128)(2,1)S(1)}, bf16[768,192]{0,1:T(8,128)(2,1)}, bf16[2,192]{1,0:T(2,128)(2,1)S(1)}) all-reduce(f32[96,20736]{1,0:T(8,128)} %reshape.310, ...), channel_id=7, replica_groups=mesh['lat'=4,'lon'=64] {'lon'}, use_global_device_ids=true, to_apply=%region_23.24.clone | all-reduce | flops 2285952 | bytes 13715712
  1123.8 8.8 collective-permute-start.12
  1132.6 6.3 collective-permute-start.13
  1140.8 8.9 collective-permute-start.15
  1159.9 4.6 concatenate.34
  1165.2 186.3 %collective-permute-start.2 = (bf16[1,8,3,12,192]{4,3,2,1,0:T(8,128)(2,1)S(1)}, bf16[1,8,3,12,192]{4,3,2,1,0:T(8,128)(2,1)S(1)}, u32[]{:S(2)}, u32[]{:S(2)}) collective-permute-start(bf16[1,8,3,12,192]{4,3,2,1,0:T(8,128)(2,1)S(1)} %fusion.27), channel_id=1, source_target_pairs={{192,0},{0,64},{64,128},{128,192},{193,1},{1,65},{65,129},{129,193... | collective-permute-start | bytes 331784 | tf_op jit(solution)/shard_map/ppermute | solution.py:16
  1351.5 39.8 %all-reduce.12.cloned.1.call-done = (bf16[16,6,324]{2,1,0:T(8,128)(2,1)}, bf16[192,9]{0,1:T(8,128)(2,1)}, bf16[192,3]{0,1:T(4,128)(2,1)}, bf16[192,12]{0,1:T(8,1...) async-done(((bf16[16,6,324]{2,1,0:T(8,128)(2,1)}, bf16[192,9]{0,1:T(8,128)(2,1)}, bf16[192,3]{0,1:T(4,128)(2,1)}, bf16[192,12]{0,1:T(8,128)(2,1)}, ...) | async-done | bytes 76060 | tf_op jit(solution)/shard_map/psum | solution.py:242
  1400.7 6.6 collective-permute-done.3
  (217 shorter events, 103.5 us)
Async XLA Ops:
  7.2 537.0 %copy-start = (s32[4,4]{1,0:T(4,128)S(1)}, s32[4,4]{1,0:T(4,128)}, u32[]{:S(2)}) copy-start(s32[4,4]{1,0:T(4,128)} %param.18) | copy-start | bytes 196
  7.2 550.8 %all-gather.7.cloned.1.call-start = ((), (), s32[]{:S(2)}) async-start(), calls=%async_computation.1 | async-start | bytes 4792320 | tf_op jit(solution)/shard_map/all_gather | solution.py:196
  10.3 535.9 %all-to-all-start = ((bf16[64,192,3]{1,2,0:T(4,128)(2,1)}), bf16[64,192,3]{1,2,0:T(4,128)(2,1)S(1)}, u32[]{:S(2)}, u32[]{:S(2)}) async-start(bf16[64,192,3]{1,2,0:T(4,128)(2,1)} %stack.32), calls=%async_computation | async-start | bytes 262144 | tf_op jit(solution)/shard_map/all_to_all | solution.py:191
  23.9 1367.4 %all-reduce.12.cloned.1.call-start = ((), (), s32[]{:S(2)}) async-start(), calls=%async_computation.2 | async-start | bytes 246784 | tf_op jit(solution)/shard_map/psum | solution.py:242
  26.6 518.6 %collective-permute-start = (bf16[2,8,3,12,192]{4,1,3,2,0:T(8,128)(2,1)S(1)}, bf16[2,8,3,12,192]{4,1,3,2,0:T(8,128)(2,1)S(1)}, u32[]{:S(2)}, u32[]{:S(2)}) collective-permute-start(bf16[2,8,3,12,192]{4,1,3,2,0:T(8,128)(2,1)S(1)} %get-tuple-element.93), channel_id=1, source_target_pairs={{64,0},{128,64},{192,128},{0,192},{65,1},{129,65},{193,129},{1,193... | collective-permute-start | bytes 663560 | tf_op jit(solution)/shard_map/ppermute | solution.py:16
  545.3 5.9 collective-permute-start.1
  745.8 375.4 %collective-permute-start.5 = (bf16[192,16]{0,1:T(8,128)(2,1)}, bf16[192,16]{0,1:T(8,128)(2,1)}, u32[]{:S(2)}, u32[]{:S(2)}) collective-permute-start(bf16[192,16]{0,1:T(8,128)(2,1)} %convert.35), channel_id=1, source_target_pairs={{0,2},{1,3},{2,4},{3,5},{4,6},{5,7},{6,8},{7,9},{8,10},{9,11},{10,... | collective-permute-start | bytes 18440
  747.7 374.8 %collective-permute-start.6 = (bf16[192,16]{0,1:T(8,128)(2,1)}, bf16[192,16]{0,1:T(8,128)(2,1)}, u32[]{:S(2)}, u32[]{:S(2)}) collective-permute-start(bf16[192,16]{0,1:T(8,128)(2,1)} %convert.35), channel_id=1, source_target_pairs={{0,3},{1,4},{2,5},{3,6},{4,7},{5,8},{6,9},{7,10},{8,11},{9,12},{10... | collective-permute-start | bytes 18440
  749.6 374.2 %collective-permute-start.7 = (bf16[192,16]{0,1:T(8,128)(2,1)}, bf16[192,16]{0,1:T(8,128)(2,1)}, u32[]{:S(2)}, u32[]{:S(2)}) collective-permute-start(bf16[192,16]{0,1:T(8,128)(2,1)} %convert.35), channel_id=1, source_target_pairs={{0,4},{1,5},{2,6},{3,7},{4,8},{5,9},{6,10},{7,11},{8,12},{9,13},{1... | collective-permute-start | bytes 18440
  751.4 381.2 %collective-permute-start.8 = (bf16[192,16]{0,1:T(8,128)(2,1)}, bf16[192,16]{0,1:T(8,128)(2,1)}, u32[]{:S(2)}, u32[]{:S(2)}) collective-permute-start(bf16[192,16]{0,1:T(8,128)(2,1)} %convert.35), channel_id=1, source_target_pairs={{0,5},{1,6},{2,7},{3,8},{4,9},{5,10},{6,11},{7,12},{8,13},{9,14},{... | collective-permute-start | bytes 18440
  770.0 348.6 %collective-permute-start.19 = (bf16[192,12]{0,1:T(8,128)(2,1)}, bf16[192,12]{0,1:T(8,128)(2,1)S(1)}, u32[]{:S(2)}, u32[]{:S(2)}) collective-permute-start(bf16[192,12]{0,1:T(8,128)(2,1)} %slice.107), channel_id=1, source_target_pairs={{0,16},{1,17},{2,18},{3,19},{4,20},{5,21},{6,22},{7,23},{8,24},{9,... | collective-permute-start | bytes 13832
  1118.6 20.3 %collective-permute-start.9 = (bf16[192,16]{0,1:T(8,128)(2,1)}, bf16[192,16]{0,1:T(8,128)(2,1)S(1)}, u32[]{:S(2)}, u32[]{:S(2)}) collective-permute-start(bf16[192,16]{0,1:T(8,128)(2,1)} %convert.35), channel_id=1, source_target_pairs={{0,6},{1,7},{2,8},{3,9},{4,10},{5,11},{6,12},{7,13},{8,14},{9,15},... | collective-permute-start | bytes 18440
  1121.2 19.6 %collective-permute-start.10 = (bf16[192,16]{0,1:T(8,128)(2,1)}, bf16[192,16]{0,1:T(8,128)(2,1)S(1)}, u32[]{:S(2)}, u32[]{:S(2)}) collective-permute-start(bf16[192,16]{0,1:T(8,128)(2,1)} %convert.35), channel_id=1, source_target_pairs={{0,7},{1,8},{2,9},{3,10},{4,11},{5,12},{6,13},{7,14},{8,15},{9,16}... | collective-permute-start | bytes 18440
  1122.5 27.2 %collective-permute-start.11 = (bf16[192,16]{0,1:T(8,128)(2,1)}, bf16[192,16]{0,1:T(8,128)(2,1)S(1)}, u32[]{:S(2)}, u32[]{:S(2)}) collective-permute-start(bf16[192,16]{0,1:T(8,128)(2,1)} %convert.35), channel_id=1, source_target_pairs={{0,8},{1,9},{2,10},{3,11},{4,12},{5,13},{6,14},{7,15},{8,16},{9,17... | collective-permute-start | bytes 18440
  1123.8 27.2 %collective-permute-start.12 = (bf16[192,16]{0,1:T(8,128)(2,1)}, bf16[192,16]{0,1:T(8,128)(2,1)S(1)}, u32[]{:S(2)}, u32[]{:S(2)}) collective-permute-start(bf16[192,16]{0,1:T(8,128)(2,1)} %convert.35), channel_id=1, source_target_pairs={{0,9},{1,10},{2,11},{3,12},{4,13},{5,14},{6,15},{7,16},{8,17},{9,1... | collective-permute-start | bytes 18440
  1132.6 20.1 %collective-permute-start.13 = (bf16[192,16]{0,1:T(8,128)(2,1)}, bf16[192,16]{0,1:T(8,128)(2,1)S(1)}, u32[]{:S(2)}, u32[]{:S(2)}) collective-permute-start(bf16[192,16]{0,1:T(8,128)(2,1)} %convert.35), channel_id=1, source_target_pairs={{0,10},{1,11},{2,12},{3,13},{4,14},{5,15},{6,16},{7,17},{8,18},{9,... | collective-permute-start | bytes 18440
  1138.9 17.8 %collective-permute-start.14 = (bf16[192,16]{0,1:T(8,128)(2,1)}, bf16[192,16]{0,1:T(8,128)(2,1)S(1)}, u32[]{:S(2)}, u32[]{:S(2)}) collective-permute-start(bf16[192,16]{0,1:T(8,128)(2,1)} %convert.35), channel_id=1, source_target_pairs={{0,11},{1,12},{2,13},{3,14},{4,15},{5,16},{6,17},{7,18},{8,19},{9,... | collective-permute-start | bytes 18440
  1140.8 19.1 %collective-permute-start.15 = (bf16[192,16]{0,1:T(8,128)(2,1)}, bf16[192,16]{0,1:T(8,128)(2,1)S(1)}, u32[]{:S(2)}, u32[]{:S(2)}) collective-permute-start(bf16[192,16]{0,1:T(8,128)(2,1)} %convert.35), channel_id=1, source_target_pairs={{0,12},{1,13},{2,14},{3,15},{4,16},{5,17},{6,18},{7,19},{8,20},{9,... | collective-permute-start | bytes 18440
  1149.7 10.2 collective-permute-start.16
  1151.0 8.9 collective-permute-start.17
  1152.7 7.2 collective-permute-start.18
  1156.8 3.1 collective-permute-start.4
  1165.2 231.3 %collective-permute-start.2 = (bf16[1,8,3,12,192]{4,3,2,1,0:T(8,128)(2,1)S(1)}, bf16[1,8,3,12,192]{4,3,2,1,0:T(8,128)(2,1)S(1)}, u32[]{:S(2)}, u32[]{:S(2)}) collective-permute-start(bf16[1,8,3,12,192]{4,3,2,1,0:T(8,128)(2,1)S(1)} %fusion.27), channel_id=1, source_target_pairs={{192,0},{0,64},{64,128},{128,192},{193,1},{1,65},{65,129},{129,193... | collective-permute-start | bytes 331784 | tf_op jit(solution)/shard_map/ppermute | solution.py:16
  1396.7 10.7 collective-permute-start.3
  (38 other events, 2590.7 us)
Sparse Core Ops, SparseCore 0:
  9.9 267.0 all-gather.6
  1165.3 225.9 all-reduce.11
